TPU v7x, 512 devices: a whole 4x4x16 slice. The times are simulated.
512 devices in a mesh: row: 64 (over x, y, z_hi, core), col: 8 (over z_lo).
Axes of the slice: x: 4, y: 4, z: 16 (z_hi: 2, z_lo: 8; z = z_hi * 8 + z_lo), core: 2. Of those that a mesh axis runs over, the one named last changes fastest.
Arguments:
- inputs: bfloat16 [256, 1024, 256], P('row', 'col'), may hold values from -6 to 6
- preactivation: bfloat16 [256, 1024, 256], P('row', 'col'), may hold values from -6 to 6
- cotangent: bfloat16 [256, 1024, 256], P('row', 'col'), may hold values from -6 to 6
- spectral: bfloat16 [2, 128, 64, 5, 1024], P(None, 'row', 'col'), may hold values from -2 to 2
- bypass: bfloat16 [32, 32], replicated, may hold values from -1 to 1
Outputs:
- grad_inputs: bfloat16 [256, 1024, 256], P('row', 'col')
- grad_spectral: float32 [2, 128, 64, 5, 1024], P(None, 'row', 'col')
- grad_bypass: float32 [32, 32], replicated
All inputs are finite; a program needn't handle non-finite values.
Results may differ from a plain program's by a relative error of at most 0.022.
Values may be sent and summed in bfloat16 or wider, within the bound.
A program may use at most 64 MiB of HBM per device.

v0:
```python
import math
import jax
import jax.numpy as jnp
from jax import lax
from jax.sharding import PartitionSpec as P

exact_mode = lax.Precision.HIGHEST


def counting(length):
    return jnp.arange(length, dtype=jnp.int32)


def kept_freq(slot_index, keep_count):
    return jnp.where(slot_index < keep_count // 2, slot_index, slot_index - keep_count)


def phase_table(outer_index, inner_index, length, direction):
    turn_count = jnp.mod(outer_index[:, None] * inner_index[None, :], length)
    angles = turn_count.astype(jnp.float32) * (2.0 * math.pi / length)
    cosine = jnp.cos(angles)
    sine_part = direction * jnp.sin(angles)
    top_rows = jnp.stack([cosine, -sine_part], axis=1)
    low_rows = jnp.stack([sine_part, cosine], axis=1)
    return jnp.stack([top_rows, low_rows], axis=0)


def time_forward(step_count, time_modes):
    turn_count = jnp.mod(counting(step_count)[:, None] * counting(time_modes)[None, :], step_count)
    angles = turn_count.astype(jnp.float32) * (2.0 * math.pi / step_count)
    return jnp.stack([jnp.cos(angles), -jnp.sin(angles)], axis=1)


def time_inverse(step_count, time_modes):
    turn_count = jnp.mod(counting(time_modes)[:, None] * counting(step_count)[None, :], step_count)
    angles = turn_count.astype(jnp.float32) * (2.0 * math.pi / step_count)
    return jnp.stack([jnp.cos(angles), -jnp.sin(angles)], axis=0)


def gelu_slope(values):
    normal_cdf = 0.5 * (1.0 + lax.erf(values * (1.0 / math.sqrt(2.0))))
    density = jnp.exp(-0.5 * values * values) * (1.0 / math.sqrt(2.0 * math.pi))
    return normal_cdf + values * density


def mix_modes(modes_in, modes_grad, weight, factor):
    in_real = modes_in[:, 0]
    in_imag = modes_in[:, 1]
    grad_real = modes_grad[:, 0]
    grad_imag = modes_grad[:, 1]
    real_part = factor * (
        in_real[..., :, None] * grad_real[..., None, :]
        + in_imag[..., :, None] * grad_imag[..., None, :]
    )
    imag_part = factor * (
        in_real[..., :, None] * grad_imag[..., None, :]
        - in_imag[..., :, None] * grad_real[..., None, :]
    )
    weight_grad = jnp.stack([real_part, imag_part], axis=0)
    w_real = weight[0]
    w_imag = weight[1]
    back_real = factor * (
        jnp.einsum("kyscd,kysd->kysc", w_real, grad_real, precision=exact_mode)
        + jnp.einsum("kyscd,kysd->kysc", w_imag, grad_imag, precision=exact_mode)
    )
    back_imag = factor * (
        jnp.einsum("kyscd,kysd->kysc", w_real, grad_imag, precision=exact_mode)
        - jnp.einsum("kyscd,kysd->kysc", w_imag, grad_real, precision=exact_mode)
    )
    return (weight_grad, jnp.stack([back_real, back_imag], axis=1))


def local(inputs, preactivation, cotangent, spectral, bypass):
    row_count, col_count, packed = inputs.shape
    chan_count = bypass.shape[0]
    step_count = packed // chan_count
    time_modes = spectral.shape[3]
    owned_row_modes = spectral.shape[1]
    owned_col_modes = spectral.shape[2]
    row_parts = lax.axis_size("row")
    col_parts = lax.axis_size("col")
    row_modes = owned_row_modes * row_parts
    col_modes = owned_col_modes * col_parts
    total_x = row_count * row_parts
    total_y = col_count * col_parts
    factor = 1.0 / math.sqrt(
        float(total_x * total_y * step_count * row_modes * col_modes * time_modes)
    )
    row_start = lax.axis_index("row") * row_count
    col_start = lax.axis_index("col") * col_count
    mode_width = owned_col_modes * time_modes * chan_count
    slopes = gelu_slope(preactivation.astype(jnp.float32))
    pre_grad = (cotangent.astype(jnp.float32) * slopes).astype(jnp.bfloat16)
    flat_inputs = inputs.reshape(-1, chan_count)
    flat_grad = pre_grad.reshape(-1, chan_count)
    local_bypass = jnp.einsum(
        "nc,nd->cd", flat_inputs, flat_grad, preferred_element_type=jnp.float32
    )
    bypass_total = lax.psum(local_bypass, ("row", "col"))
    grad_bypass = bypass_total * (1.0 / math.sqrt(float(total_x * total_y * step_count)))
    forward_t = time_forward(step_count, time_modes)
    col_table = phase_table(counting(col_modes), col_start + counting(col_count), total_y, -1.0)

    def column_terms(field):
        cube_view = field.astype(jnp.float32).reshape(row_count, col_count, step_count, chan_count)
        in_time = jnp.einsum("rytc,tqs->ryqsc", cube_view, forward_t, precision=exact_mode)
        return jnp.einsum("akpy,rypsc->raksc", col_table, in_time, precision=exact_mode)

    col_in, col_grad = (
        lax.psum_scatter(
            column_terms(inputs).astype(jnp.bfloat16), "col", scatter_dimension=2, tiled=True
        ).astype(jnp.float32),
        lax.psum_scatter(
            column_terms(pre_grad).astype(jnp.bfloat16), "col", scatter_dimension=2, tiled=True
        ).astype(jnp.float32),
    )
    flat_in = col_in.reshape(row_count, 2, mode_width)
    flat_cols = col_grad.reshape(row_count, 2, mode_width)
    stacked = jnp.stack([flat_in, flat_cols], axis=2)
    frequencies = kept_freq(counting(owned_row_modes * lax.axis_size("row")), row_modes)
    phases = phase_table(frequencies, row_start + counting(row_count), total_x, -1.0)
    owned_modes = lax.psum_scatter(
        jnp.einsum("akpr,rpbm->kabm", phases, stacked, precision=exact_mode),
        "row",
        scatter_dimension=0,
        tiled=True,
    )
    modes_in = owned_modes[:, :, 0]
    modes_grad = owned_modes[:, :, 1]
    mode_shape = (owned_row_modes, 2, owned_col_modes, time_modes, chan_count)
    weight = spectral.astype(jnp.float32).reshape(
        2, owned_row_modes, owned_col_modes, time_modes, chan_count, chan_count
    )
    weight_grad, back_modes = mix_modes(
        modes_in.reshape(mode_shape), modes_grad.reshape(mode_shape), weight, factor
    )
    grad_spectral = weight_grad.reshape(spectral.shape)
    flat_back = back_modes.reshape(owned_row_modes, 2, mode_width)
    mode_piece = lax.all_gather(flat_back, "row", axis=0, tiled=True)
    span_count = mode_piece.shape[0]
    frequencies = kept_freq(counting(span_count), row_modes)
    phases = phase_table(row_start + counting(row_count), frequencies, total_x, 1.0)
    rows_back = jnp.einsum("axpk,kpm->xam", phases, mode_piece, precision=exact_mode)
    rows_view = rows_back.reshape(row_count, 2, owned_col_modes, time_modes, chan_count)
    col_piece = lax.all_gather(rows_view.astype(jnp.bfloat16), "col", axis=2, tiled=True).astype(
        jnp.float32
    )
    span_count = col_piece.shape[2]
    phases = phase_table(col_start + counting(col_count), counting(span_count), total_y, 1.0)
    cells_y = jnp.zeros(
        (row_count, col_count, 2, time_modes, chan_count), jnp.float32
    ) + jnp.einsum("aypk,rpksc->ryasc", phases, col_piece, precision=exact_mode)
    kernel_grad = jnp.einsum(
        "ryasc,ast->rytc", cells_y, time_inverse(step_count, time_modes), precision=exact_mode
    )
    bypass_grad = jnp.einsum("nd,cd->nc", flat_grad, bypass, preferred_element_type=jnp.float32)
    total_grad = kernel_grad.reshape(-1, chan_count) + bypass_grad
    grad_inputs = total_grad.reshape(inputs.shape).astype(jnp.bfloat16)
    return (grad_inputs, grad_spectral, grad_bypass)


def solution(mesh):
    return jax.shard_map(
        local,
        mesh=mesh,
        in_specs=(
            P("row", "col", None),
            P("row", "col", None),
            P("row", "col", None),
            P(None, "row", "col", None, None),
            P(),
        ),
        out_specs=(P("row", "col", None), P(None, "row", "col", None, None), P()),
        check_vma=False,
    )
```

profile of v0, /device:TPU:4, one launch (start us, length us, event | category | flops | bytes accessed | tf_op | source)
XLA Modules:
  0.0 1429.1 jit_solution(1506078009365955725)
XLA Ops:
  7.5 1.1 copy.63
  8.6 1.1 copy.64
  10.6 0.7 fusion.7
  11.3 1.2 copy.67
  13.3 0.7 fusion.8
  14.0 1.2 copy.61
  15.3 1.3 dynamic-slice
  17.3 133.3 %all-reduce.9.cloned.1.call-done = (bf16[4,2,64,5,32]{4,0,3,1,2:T(4,128)(2,1)}, bf16[4,2,64,5,32]{4,0,3,1,2:T(4,128)(2,1)}) async-done(((bf16[4,2,64,5,32]{4,0,3,1,2:T(4,128)(2,1)}, bf16[4,2,64,5,32]{4,0,3,1,2:T(4,128)(2,1)}), (bf16[4,2,64,5,32]{4,0,3,1,2:T(4,128)(2,1)}, bf16[4,2,64,5,32]{4,0,3,1,2:T(4,128)(2,1)})) %all-reduce.9.cloned.1.call-update) | async-done | bytes 327696
  150.6 0.9 constant_dynamic-slice_fusion.1
  151.7 0.9 constant_dynamic-slice_fusion
  152.8 1.2 convolution_bitcast_fusion
  154.0 3.3 copy.71
  157.4 1.3 dynamic-slice.4
  160.3 1045.6 %all-reduce.7.cloned.1.call-done = f32[128,2,2,1280]{3,2,1,0:T(2,128)} async-done(((f32[128,2,2,1280]{3,2,1,0:T(2,128)}), f32[128,2,2,1280]{3,2,1,0:T(2,128)}) %all-reduce.7.cloned.1.call-update) | async-done | bytes 2621456
  1205.9 1.0 dynamic-slice_reduce_fusion
  1207.0 1.1 fusion.19
  1208.2 1.1 fusion.17
  1209.3 1.1 fusion.15
  1210.4 1.1 fusion.13
  1213.9 145.5 %psum.7 = f32[32,32]{0,1:T(8,128)S(1)} all-reduce(f32[32,32]{0,1:T(8,128)S(1)} %convolution_bitcast_fusion.8), channel_id=1, replica_groups=mesh['row'=64,'col'=8] {'row','col'}, use_global_device_ids=true, to_apply=%region_3.4 | all-reduce | flops 1024 | bytes 8192 | tf_op jit(solution)/shard_map/psum | solution.py:99
  1359.4 0.7 copy.85
  1360.7 1.7 add_multiply_fusion
  1362.4 1.9 mul.549
  1364.9 0.9 pad_maximum_fusion
  1365.8 2.1 fusion.2
  1368.1 45.4 %all_gather.7 = bf16[4,2,64,5,32]{4,2,1,3,0:T(8,128)(2,1)S(1)} all-gather(bf16[4,2,8,5,32]{4,2,1,3,0:T(8,128)(2,1)S(1)} %copy.75), channel_id=1, replica_groups=mesh['row'=64,'col'=8] {'col'}, dimensions={2}, use_global_device_ids=true | all-gather | bytes 184320 | tf_op jit(solution)/shard_map/all_gather | solution.py:145
  1413.4 0.7 convolution_bitcast_fusion.4
  1414.1 1.8 convolution_bitcast_fusion.7
  1416.0 1.7 copy.77
  1417.7 1.4 copy.79
  1419.1 1.5 fusion
  1421.1 1.4 convert_element_type.163
  (60 shorter events, 7.6 us)
Async XLA Ops:
  7.2 1412.0 %copy-start = (bf16[32,32]{1,0:T(8,128)(2,1)S(1)}, bf16[32,32]{1,0:T(8,128)(2,1)}, u32[]{:S(2)}) copy-start(bf16[32,32]{1,0:T(8,128)(2,1)} %param.9) | copy-start | bytes 6148
  7.2 143.4 %all-reduce.9.cloned.1.call-start = ((), (), s32[]{:S(2)}) async-start(), calls=%async_computation.2 | async-start | bytes 2621440
  10.6 1.9 copy-start.1
  15.2 1190.7 %all-reduce.7.cloned.1.call-start = ((), (), s32[]{:S(2)}) async-start(), calls=%async_computation.1 | async-start | bytes 5242880
  157.3 1.4 copy-start.2
  157.4 1208.4 %all-gather.2.cloned.1.call-start = ((), (), s32[]{:S(2)}) async-start(), calls=%async_computation | async-start | bytes 1331200 | tf_op jit(solution)/shard_map/all_gather | solution.py:139
Sparse Core Ops, SparseCore 0:
  15.3 135.2 all-reduce.8
  157.5 1048.3 all-reduce.6
  1212.6 139.5 all-gather.1
where the time goes:
time: 1430 us
  waiting for transfers between devices  1180 us (83%)
  blocking collectives  191 us (13%)
  local copies, waits for them, and re-layouts  25.2 us (2%)
  between operations  15.4 us (1%)
  matrix products  14.9 us (1%)
    unnamed x5, waiting for transfers between devices  1180 us
    psum x1, blocking collectives, local(): bypass_total = lax.psum(local_bypass, ('row', 'col'))  146 us
    all_gather x1, blocking collectives, local(): lax.all_gather(rows_view.astype(jnp.bfloat16), 'col', axis=2, tiled=True)  45.4 us
  transfers between devices with their start and end apart: 3, of which 2 were waited for; matrix products, arithmetic and copies ran while one was open for 1% of the time, Pallas kernels for 0%

commit v1 on v0

--- a/solution.py
+++ b/solution.py
@@ -96,7 +96,7 @@
     local_bypass = jnp.einsum(
         "nc,nd->cd", flat_inputs, flat_grad, preferred_element_type=jnp.float32
     )
-    bypass_total = lax.psum(local_bypass, ("row", "col"))
+    bypass_total = lax.psum(lax.psum(local_bypass, "row"), "col")
     grad_bypass = bypass_total * (1.0 / math.sqrt(float(total_x * total_y * step_count)))
     forward_t = time_forward(step_count, time_modes)
     col_table = phase_table(counting(col_modes), col_start + counting(col_count), total_y, -1.0)

time: 1430 us -> 1930 us (1.35)
  the two profiles are of different devices: /device:TPU:4 before, /device:TPU:0 now
where the time goes in v1:
time: 1930 us
  waiting for transfers between devices  1210 us (63%)
  blocking collectives  664 us (34%)
  local copies, waits for them, and re-layouts  25.2 us (1%)
    unnamed x5, waiting for transfers between devices  1210 us
    psum x2, blocking collectives, local(): bypass_total = lax.psum(lax.psum(local_bypass, 'row'), 'col')  620 us
    all_gather x1, blocking collectives, local(): lax.all_gather(rows_view.astype(jnp.bfloat16), 'col', axis=2, tiled=True)  44.5 us
  transfers between devices with their start and end apart: 3, of which 2 were waited for; matrix products, arithmetic and copies ran while one was open for 1% of the time, Pallas kernels for 0%

profile of v1, /device:TPU:0, one launch (start us, length us, event | category | flops | bytes accessed | tf_op | source)
XLA Modules:
  0.0 1931.6 jit_solution(11660759642615103840)
XLA Ops:
  7.5 1.1 copy.63
  8.6 1.1 copy.64
  10.6 0.7 fusion.7
  11.3 1.2 copy.67
  13.3 0.7 fusion.8
  14.0 1.2 copy.61
  15.3 1.3 dynamic-slice
  17.3 127.9 %all-reduce.9.cloned.1.call-done = (bf16[4,2,64,5,32]{4,0,3,1,2:T(4,128)(2,1)}, bf16[4,2,64,5,32]{4,0,3,1,2:T(4,128)(2,1)}) async-done(((bf16[4,2,64,5,32]{4,0,3,1,2:T(4,128)(2,1)}, bf16[4,2,64,5,32]{4,0,3,1,2:T(4,128)(2,1)}), (bf16[4,2,64,5,32]{4,0,3,1,2:T(4,128)(2,1)}, bf16[4,2,64,5,32]{4,0,3,1,2:T(4,128)(2,1)})) %all-reduce.9.cloned.1.call-update) | async-done | bytes 327696
  145.3 0.9 constant_dynamic-slice_fusion.1
  146.4 0.9 constant_dynamic-slice_fusion
  147.5 1.2 convolution_bitcast_fusion
  148.7 3.3 copy.71
  152.1 1.3 dynamic-slice.4
  155.0 1080.0 %all-reduce.7.cloned.1.call-done = f32[128,2,2,1280]{3,2,1,0:T(2,128)} async-done(((f32[128,2,2,1280]{3,2,1,0:T(2,128)}), f32[128,2,2,1280]{3,2,1,0:T(2,128)}) %all-reduce.7.cloned.1.call-update) | async-done | bytes 2621456
  1234.9 1.0 dynamic-slice_reduce_fusion
  1236.0 1.1 fusion.19
  1237.1 1.1 fusion.17
  1238.3 1.1 fusion.15
  1239.4 1.1 fusion.13
  1242.9 568.5 %psum.14 = f32[32,32]{0,1:T(8,128)S(1)} all-reduce(f32[32,32]{0,1:T(8,128)S(1)} %convolution_bitcast_fusion.8), channel_id=1, replica_groups=mesh['row'=64,'col'=8] {'row'}, use_global_device_ids=true, to_apply=%region_3.4 | all-reduce | flops 1024 | bytes 8192 | tf_op jit(solution)/shard_map/psum | solution.py:99
  1811.4 51.3 %psum.15 = f32[32,32]{0,1:T(8,128)S(1)} all-reduce(f32[32,32]{0,1:T(8,128)S(1)} %psum.14), channel_id=1, replica_groups=mesh['row'=64,'col'=8] {'col'}, use_global_device_ids=true, to_apply=%region_4.5 | all-reduce | flops 1024 | bytes 8192 | tf_op jit(solution)/shard_map/psum | solution.py:99
  1864.0 1.7 add_multiply_fusion
  1865.7 1.9 mul.549
  1868.2 0.9 pad_maximum_fusion
  1869.1 2.1 fusion.2
  1871.4 44.5 %all_gather.7 = bf16[4,2,64,5,32]{4,2,1,3,0:T(8,128)(2,1)S(1)} all-gather(bf16[4,2,8,5,32]{4,2,1,3,0:T(8,128)(2,1)S(1)} %copy.75), channel_id=1, replica_groups=mesh['row'=64,'col'=8] {'col'}, dimensions={2}, use_global_device_ids=true | all-gather | bytes 184320 | tf_op jit(solution)/shard_map/all_gather | solution.py:145
  1915.9 0.7 convolution_bitcast_fusion.4
  1916.6 1.8 convolution_bitcast_fusion.7
  1918.5 1.7 copy.77
  1920.2 1.4 copy.79
  1921.6 1.5 fusion
  1923.6 1.4 convert_element_type.163
  (61 shorter events, 8.3 us)
Async XLA Ops:
  7.2 1914.5 %copy-start = (bf16[32,32]{1,0:T(8,128)(2,1)S(1)}, bf16[32,32]{1,0:T(8,128)(2,1)}, u32[]{:S(2)}) copy-start(bf16[32,32]{1,0:T(8,128)(2,1)} %param.9) | copy-start | bytes 6148
  7.2 138.1 %all-reduce.9.cloned.1.call-start = ((), (), s32[]{:S(2)}) async-start(), calls=%async_computation.2 | async-start | bytes 2621440
  10.6 1.9 copy-start.1
  15.2 1219.7 %all-reduce.7.cloned.1.call-start = ((), (), s32[]{:S(2)}) async-start(), calls=%async_computation.1 | async-start | bytes 5242880
  152.0 1.4 copy-start.2
  152.0 1717.1 %all-gather.2.cloned.1.call-start = ((), (), s32[]{:S(2)}) async-start(), calls=%async_computation | async-start | bytes 1331200 | tf_op jit(solution)/shard_map/all_gather | solution.py:139
Sparse Core Ops, SparseCore 0:
  15.3 129.9 all-reduce.8
  152.2 1082.6 all-reduce.6
  1241.6 106.1 all-gather.1

commit v2 on v0

--- a/solution.py
+++ b/solution.py
@@ -96,7 +96,7 @@
     local_bypass = jnp.einsum(
         "nc,nd->cd", flat_inputs, flat_grad, preferred_element_type=jnp.float32
     )
-    bypass_total = lax.psum(local_bypass, ("row", "col"))
+    bypass_total = jnp.sum(lax.all_gather(local_bypass, ("row", "col")), axis=0)
     grad_bypass = bypass_total * (1.0 / math.sqrt(float(total_x * total_y * step_count)))
     forward_t = time_forward(step_count, time_modes)
     col_table = phase_table(counting(col_modes), col_start + counting(col_count), total_y, -1.0)

time: 1430 us -> 1800 us (1.26)
  the two profiles are of different devices: /device:TPU:4 before, /device:TPU:2 now
where the time goes in v2:
time: 1800 us; the launch traced here: 1790 us
  waiting for transfers between devices  1680 us (93%)
  blocking collectives  45.4 us (3%)
  local copies, waits for them, and re-layouts  25.9 us (1%)
    unnamed x6, waiting for transfers between devices  1180 us
    all_gather x1, waiting for transfers between devices, local(): bypass_total = jnp.sum(lax.all_gather(local_bypass, ('row', 'col')), axis=0)  400 us
    all_gather x1, waiting for transfers between devices, local(): mode_piece = lax.all_gather(flat_back, 'row', axis=0, tiled=True)  105 us
    all_gather x1, blocking collectives, local(): lax.all_gather(rows_view.astype(jnp.bfloat16), 'col', axis=2, tiled=True)  45.4 us
  transfers between devices with their start and end apart: 4, of which 4 were waited for; matrix products, arithmetic and copies ran while one was open for 1% of the time, Pallas kernels for 0%

profile of v2, /device:TPU:2, one launch (start us, length us, event | category | flops | bytes accessed | tf_op | source)
XLA Modules:
  0.0 1794.6 jit_solution(10919044804261258862)
XLA Ops:
  8.3 1.1 copy.63
  9.4 1.1 copy.64
  11.4 0.7 fusion.7
  12.2 1.2 copy.67
  14.1 0.7 fusion.8
  14.8 1.2 copy.61
  16.1 1.3 dynamic-slice
  18.2 133.5 %all-reduce.9.cloned.1.call-done = (bf16[4,2,64,5,32]{4,0,3,1,2:T(4,128)(2,1)}, bf16[4,2,64,5,32]{4,0,3,1,2:T(4,128)(2,1)}) async-done(((bf16[4,2,64,5,32]{4,0,3,1,2:T(4,128)(2,1)}, bf16[4,2,64,5,32]{4,0,3,1,2:T(4,128)(2,1)}), (bf16[4,2,64,5,32]{4,0,3,1,2:T(4,128)(2,1)}, bf16[4,2,64,5,32]{4,0,3,1,2:T(4,128)(2,1)})) %all-reduce.9.cloned.1.call-update) | async-done | bytes 327696
  151.7 0.9 constant_dynamic-slice_fusion.1
  152.8 0.9 constant_dynamic-slice_fusion
  153.9 1.2 convolution_bitcast_fusion
  155.1 3.3 copy.71
  160.9 1.3 dynamic-slice.4
  163.7 1045.1 %all-reduce.7.cloned.1.call-done = f32[128,2,2,1280]{3,2,1,0:T(2,128)} async-done(((f32[128,2,2,1280]{3,2,1,0:T(2,128)}), f32[128,2,2,1280]{3,2,1,0:T(2,128)}) %all-reduce.7.cloned.1.call-update) | async-done | bytes 2621456
  1208.8 1.0 dynamic-slice_reduce_fusion
  1209.9 1.1 fusion.19
  1211.0 1.1 fusion.15
  1212.3 1.1 fusion.17
  1213.4 1.1 fusion.13
  1215.9 1.7 add_multiply_fusion
  1217.6 1.9 mul.549
  1220.1 0.9 pad_maximum_fusion
  1221.0 399.5 %all-gather.6.cloned.1.call-done = f32[16384,32]{1,0:T(8,128)} async-done(((f32[32,32]{1,0:T(8,128)}), f32[16384,32]{1,0:T(8,128)}) %all-gather.6.cloned.1.call-update) | async-done | bytes 2097168 | tf_op jit(solution)/shard_map/all_gather | solution.py:99
  1620.5 4.0 reduce_sum.9
  1625.3 105.1 %all-gather.4.cloned.1.call-done = f32[128,2,1280]{2,1,0:T(2,128)} async-done(((f32[2,2,1280]{2,1,0:T(2,128)}), f32[128,2,1280]{2,1,0:T(2,128)}) %all-gather.4.cloned.1.call-update) | async-done | bytes 1310736 | tf_op jit(solution)/shard_map/all_gather | solution.py:139
  1730.3 2.1 fusion.2
  1732.6 45.4 %all_gather.13 = bf16[4,2,64,5,32]{4,2,1,3,0:T(8,128)(2,1)S(1)} all-gather(bf16[4,2,8,5,32]{4,2,1,3,0:T(8,128)(2,1)S(1)} %copy.75), channel_id=1, replica_groups=mesh['row'=64,'col'=8] {'col'}, dimensions={2}, use_global_device_ids=true | all-gather | bytes 184320 | tf_op jit(solution)/shard_map/all_gather | solution.py:145
  1778.8 1.8 convolution_bitcast_fusion.7
  1780.6 1.7 copy.77
  1782.4 1.4 copy.79
  1783.7 1.5 fusion
  1785.7 1.4 convert_element_type.163
  (65 shorter events, 10.0 us)
Async XLA Ops:
  8.0 1775.7 %copy-start = (bf16[32,32]{1,0:T(8,128)(2,1)S(1)}, bf16[32,32]{1,0:T(8,128)(2,1)}, u32[]{:S(2)}) copy-start(bf16[32,32]{1,0:T(8,128)(2,1)} %param.9) | copy-start | bytes 6148
  8.0 143.6 %all-reduce.9.cloned.1.call-start = ((), (), s32[]{:S(2)}) async-start(), calls=%async_computation.3 | async-start | bytes 2621440
  11.4 1.9 copy-start.1
  16.0 1192.8 %all-reduce.7.cloned.1.call-start = ((), (), s32[]{:S(2)}) async-start(), calls=%async_computation.2 | async-start | bytes 5242880
  158.4 1462.1 %all-gather.6.cloned.1.call-start = ((), (), s32[]{:S(2)}) async-start(), calls=%async_computation.1 | async-start | bytes 8404992 | tf_op jit(solution)/shard_map/all_gather | solution.py:99
  159.5 2.7 copy-start.2
  160.7 1569.7 %all-gather.4.cloned.1.call-start = ((), (), s32[]{:S(2)}) async-start(), calls=%async_computation | async-start | bytes 1331200 | tf_op jit(solution)/shard_map/all_gather | solution.py:139
Sparse Core Ops, SparseCore 0:
  16.1 135.4 all-reduce.8
  158.5 1050.2 all-reduce.6
Sparse Core Ops, SparseCore 1:
  161.7 1458.8 all-gather.5
  1626.1 104.2 all-gather.3
